TPU v7x, 512 devices: a whole 4x8x8 slice. The times are simulated.
512 devices in a mesh: aa: 8 (over x, core), ba: 8 (over y), col: 8 (over z).
Axes of the slice: x: 4, y: 8, z: 8, core: 2. Of those that a mesh axis runs over, the one named last changes fastest.
Arguments:
- field: float32 [192, 1024, 1024], P('col', 'aa', 'ba'), may hold values from -6 to 6
- factor: float32 [1024, 256], P('aa'), may hold values from -0.1875 to 0.1875
Outputs:
- gram: float32 [1024, 1024], P('ba', ('aa', 'col'))
All inputs are finite; a program needn't handle non-finite values.
Results may differ from a plain program's by a relative error of at most 0.000076.
Values sent between devices are 32-bit elements; how exact they have to be, the bound alone decides.
A program may use at most 64 MiB of HBM per device.

v0:
```python
import jax
import jax.numpy as jnp
from jax import lax
from jax.sharding import PartitionSpec as P


def shards(field, factor):
    ranks = factor.shape[1]
    depth = field.shape[0] * lax.axis_size("col")
    partial_core = jnp.einsum("kab,ar->krb", field, factor, precision=lax.Precision.HIGHEST)
    core = lax.psum_scatter(partial_core, "aa", scatter_dimension=1, tiled=True)
    block = jnp.einsum(
        "krb,krc->bc",
        core,
        lax.all_gather(core, "ba", axis=2, tiled=True),
        precision=lax.Precision.HIGHEST,
    )
    summed = lax.psum_scatter(block, ("aa", "col"), scatter_dimension=1, tiled=True)
    return summed / jnp.sqrt(jnp.float32(ranks * depth))


def solution(mesh):
    placed = (P("col", "aa", "ba"), P("aa", None))
    return jax.shard_map(
        shards, mesh=mesh, in_specs=placed, out_specs=P("ba", ("aa", "col")), check_vma=False
    )
```

profile of v0, /device:TPU:8, one launch (start us, length us, event | category | flops | bytes accessed | tf_op | source)
XLA Modules:
  0.0 328.2 jit_solution(14949219071277259198)
XLA Ops:
  6.5 0.0 copy-start
  6.5 0.0 reduce-scatter.2.cloned.1.call-start
  6.5 1.4 copy-done
  7.9 5.2 %convolution_bitcast_fusion = f32[24,256,128]{2,1,0:T(8,128)} fusion(f32[24,128,128]{2,1,0:T(8,128)S(1)} %copy-done, f32[128,256]{1,0:T(8,128)} %param.3), kind=kOutput, calls=%fused_computation | convolution fusion | flops 1207959552 | bytes 4849664 | tf_op jit(solution)/shard_map/kab,ar->krb/dot_general | solution.py:10
  13.2 0.0 reduce-scatter.2.cloned.1.call-update
  13.2 0.0 all-gather.2.cloned.1.call-start
  13.2 45.9 %reduce-scatter.2.cloned.1.call-done = f32[24,32,128]{2,1,0:T(8,128)} async-done(((f32[24,256,128]{2,1,0:T(8,128)}), f32[24,32,128]{2,1,0:T(8,128)}) %reduce-scatter.2.cloned.1.call-update) | async-done | bytes 393232 | tf_op jit(solution)/shard_map/reduce_scatter | solution.py:11
  59.1 0.0 all-gather.2.cloned.1.call-update
  59.2 0.0 all-reduce.3.cloned.1.call-start
  59.2 59.3 %all-gather.2.cloned.1.call-done = f32[24,32,1024]{2,1,0:T(8,128)} async-done(((f32[24,32,128]{2,1,0:T(8,128)}), f32[24,32,1024]{2,1,0:T(8,128)}) %all-gather.2.cloned.1.call-update) | async-done | bytes 3145744 | tf_op jit(solution)/shard_map/all_gather | solution.py:15
  118.5 7.9 %convolution_bitcast_fusion.1 = f32[128,1024]{0,1:T(8,128)} fusion(f32[24,32,128]{2,1,0:T(8,128)} %reduce-scatter.2.cloned.1.call-done, f32[24,32,1024]{2,1,0:T(8,128)} %all-gather.2.cloned.1.call-done), kind=kOutput, calls=%fused_computation.1 | convolution fusion | flops 1207959552 | bytes 4063232 | tf_op jit(solution)/shard_map/krb,krc->bc/dot_general | solution.py:12
  126.4 0.0 all-reduce.3.cloned.1.call-update
  126.4 1.3 dynamic-slice
  128.3 192.1 %all-reduce.3.cloned.1.call-done = f32[128,1024]{0,1:T(8,128)} async-done(((f32[128,1024]{0,1:T(8,128)}), f32[128,1024]{0,1:T(8,128)}) %all-reduce.3.cloned.1.call-update) | async-done | bytes 524304
  320.4 1.3 dynamic-slice_multiply_fusion
Async XLA Ops:
  6.5 1.4 copy-start
  6.5 52.6 %reduce-scatter.2.cloned.1.call-start = ((), (), s32[]{:S(2)}) async-start(), calls=%async_computation.1 | async-start | bytes 3538944 | tf_op jit(solution)/shard_map/reduce_scatter | solution.py:11
  13.2 105.3 %all-gather.2.cloned.1.call-start = ((), (), s32[]{:S(2)}) async-start(), calls=%async_computation.2 | async-start | bytes 3538944 | tf_op jit(solution)/shard_map/all_gather | solution.py:15
  59.2 261.2 %all-reduce.3.cloned.1.call-start = ((), (), s32[]{:S(2)}) async-start(), calls=%async_computation.3 | async-start | bytes 1048576
Sparse Core Ops, SparseCore 0:
  13.3 45.7 reduce-scatter.1
  61.1 57.3 all-gather.1
  126.5 193.8 all-reduce.2
where the time goes:
time: 328 us
  waiting for transfers between devices  297 us (91%)
  between operations  13.8 us (4%)
  matrix products  13.1 us (4%)
    unnamed x4, waiting for transfers between devices  192 us
    all_gather x1, waiting for transfers between devices, shards(): lax.all_gather(core, 'ba', axis=2, tiled=True)  59.3 us
    reduce_scatter x1, waiting for transfers between devices, shards(): core = lax.psum_scatter(partial_core, 'aa', scatter_dimension=1, tiled=True)  45.9 us
    dot_general x1, matrix products, shards(): jnp.einsum('krb,krc->bc', core, lax.all_gather(core, 'ba', axis=2, tiled=...  7.85 us
  transfers between devices with their start and end apart: 3, of which 3 were waited for; matrix products, arithmetic and copies ran while one was open for 0% of the time, Pallas kernels for 0%

commit v1 on v0

--- a/solution.py
+++ b/solution.py
@@ -12,7 +12,9 @@
     block = jnp.einsum(
         "krb,krc->bc",
         core,
-        lax.all_gather(core, "ba", axis=2, tiled=True),
+        jnp.concatenate(
+            lax.all_to_all(jnp.stack([core] * lax.axis_size("ba")), "ba", 0, 0), axis=2
+        ),
         precision=lax.Precision.HIGHEST,
     )
     summed = lax.psum_scatter(block, ("aa", "col"), scatter_dimension=1, tiled=True)

time: 328 us -> 345 us (1.052)
  blocking collectives: 0 us -> 76.6 us
  waiting for transfers between devices: 297 us -> 237 us
    all_to_all x0 -> x1, blocking collectives: none -> 76.6 us  [shards(): lax.all_to_all(jnp.stack([core] * lax.axis_size('ba')), 'ba', 0, 0)]
    all_gather x1 -> x0, waiting for transfers between devices: 59.3 us -> none  [shards(): lax.all_gather(core, 'ba', axis=2, tiled=True)]
    unnamed x4 -> x3, waiting for transfers between devices: 192 us -> 191 us
  transfers between devices with their start and end apart: 3 -> 2, of which waited for: 3 -> 2; matrix products, arithmetic and copies ran while one was open for 0% -> 0% of each run, Pallas kernels for 0% -> 0%
where the time goes in v1:
time: 345 us
  waiting for transfers between devices  237 us (69%)
  blocking collectives  76.6 us (22%)
  between operations  14.1 us (4%)
  matrix products  11.2 us (3%)
  local copies, waits for them, and re-layouts  4.07 us (1%)
    unnamed x3, waiting for transfers between devices  191 us
    all_to_all x1, blocking collectives, shards(): lax.all_to_all(jnp.stack([core] * lax.axis_size('ba')), 'ba', 0, 0)  76.6 us
    reduce_scatter x1, waiting for transfers between devices, shards(): core = lax.psum_scatter(partial_core, 'aa', scatter_dimension=1, tiled=True)  45.9 us
  transfers between devices with their start and end apart: 2, of which 2 were waited for; matrix products, arithmetic and copies ran while one was open for 0% of the time, Pallas kernels for 0%

profile of v1, /device:TPU:8, one launch (start us, length us, event | category | flops | bytes accessed | tf_op | source)
XLA Modules:
  0.0 344.5 jit_solution(8758493183253980953)
XLA Ops:
  6.5 0.0 copy-start
  6.5 0.0 reduce-scatter.2.cloned.1.call-start
  6.5 1.4 copy-done
  7.9 5.2 %convolution_bitcast_fusion = f32[24,256,128]{2,1,0:T(8,128)} fusion(f32[24,128,128]{2,1,0:T(8,128)S(1)} %copy-done, f32[128,256]{1,0:T(8,128)} %param.3), kind=kOutput, calls=%fused_computation.3 | convolution fusion | flops 1207959552 | bytes 4849664 | tf_op jit(solution)/shard_map/kab,ar->krb/dot_general | solution.py:10
  13.2 0.0 reduce-scatter.2.cloned.1.call-update
  13.2 0.0 all-reduce.3.cloned.1.call-start
  13.2 45.9 %reduce-scatter.2.cloned.1.call-done = f32[24,32,128]{2,1,0:T(8,128)} async-done(((f32[24,256,128]{2,1,0:T(8,128)}), f32[24,32,128]{2,1,0:T(8,128)}) %reduce-scatter.2.cloned.1.call-update) | async-done | bytes 393232 | tf_op jit(solution)/shard_map/reduce_scatter | solution.py:11
  59.2 1.4 stack.2
  60.5 0.0 copy-start.1
  60.6 76.6 %all_to_all.5 = f32[8,24,32,128]{3,2,1,0:T(8,128)S(1)} all-to-all(f32[8,24,32,128]{3,2,1,0:T(8,128)S(1)} %stack.2), channel_id=1, replica_groups=mesh['aa'=8,'ba'=8,'col'=8] {'ba'}, dimensions={0} | all-to-all | bytes 6291456 | tf_op jit(solution)/shard_map/all_to_all | solution.py:16
  137.2 0.0 copy-done.1
  137.2 6.0 %fusion.3 = f32[128,1024]{0,1:T(8,128)} fusion(f32[24,32,128]{2,1,0:T(8,128)S(1)} %copy-done.1, f32[8,24,32,128]{3,2,1,0:T(8,128)S(1)} %all_to_all.5), kind=kOutput, calls=%fused_computation.4 | convolution fusion | flops 1207959552 | bytes 4063232 | tf_op jit(solution)/shard_map/krb,krc->bc/dot_general | solution.py:12
  143.1 0.0 all-reduce.3.cloned.1.call-update
  143.2 1.3 dynamic-slice
  145.1 191.3 %all-reduce.3.cloned.1.call-done = f32[128,1024]{0,1:T(8,128)} async-done(((f32[128,1024]{0,1:T(8,128)}), f32[128,1024]{0,1:T(8,128)}) %all-reduce.3.cloned.1.call-update) | async-done | bytes 524304
  336.4 1.3 dynamic-slice_multiply_fusion
Async XLA Ops:
  6.5 1.4 copy-start
  6.5 52.6 %reduce-scatter.2.cloned.1.call-start = ((), (), s32[]{:S(2)}) async-start(), calls=%async_computation.2 | async-start | bytes 3538944 | tf_op jit(solution)/shard_map/reduce_scatter | solution.py:11
  13.2 323.2 %all-reduce.3.cloned.1.call-start = ((), (), s32[]{:S(2)}) async-start(), calls=%async_computation.3 | async-start | bytes 1048576
  60.5 76.6 %copy-start.1 = (f32[24,32,128]{2,1,0:T(8,128)S(1)}, f32[24,32,128]{2,1,0:T(8,128)}, u32[]{:S(2)}) copy-start(f32[24,32,128]{2,1,0:T(8,128)} %reduce-scatter.2.cloned.1.call-done) | copy-start | bytes 1179652
Sparse Core Ops, SparseCore 0:
  13.3 45.7 reduce-scatter.1
  143.3 193.0 all-reduce.2
